TPU v7x, 32 devices: a whole 2x2x4 slice. The times are simulated.
32 devices in a mesh: groups: 2 (over y), patch: 4 (over z), sub: 2 (over x), half: 2 (over core).
Axes of the slice: x: 2, y: 2, z: 4, core: 2. Of those that a mesh axis runs over, the one named last changes fastest.
Arguments:
- vectors: float32 [2, 8192, 256], P(None, ('groups', 'patch', 'sub', 'half')), parts along dimension 1, may hold values from -600 to 600
- prestress: bfloat16 [8192, 3, 256], P(('groups', 'patch', 'sub', 'half')), parts along dimension 0, may hold values from -4 to 4
- thickness: float32 [8192, 256], P(('groups', 'patch', 'sub', 'half')), parts along dimension 0, may hold values from 0.5 to 2
- foundation: float32 [8192, 256], P(('groups', 'patch', 'sub', 'half')), parts along dimension 0, may hold values from 2 to 6
- patch_rows: int32 [64], P(('groups', 'patch', 'sub', 'half')), parts along dimension 0, may hold values from 64 to 128, as said below
- matched: int32 [64], P(('groups', 'patch', 'sub', 'half')), parts along dimension 0, may hold values from 0 to 31, as said below
- elem_row: int32 [8192], P(('groups', 'patch', 'sub', 'half')), parts along dimension 0, may hold values from 0 to 4095, as said below
Outputs:
- modes: float32 [2, 8192, 256], P(None, ('groups', 'patch', 'sub', 'half')), parts along dimension 1
There are 2 independent parts, one for each index of `groups`. A program takes and returns all parts, laid end to end along the dimension named above; each array names one. Nothing has to cross between parts.
Inputs may be any that keep to these rules, and one draw needn't show every extreme that they name: `patch_rows`: the largest value is reached by some patch in every draw. A permutation of the patches; the patch matched to a patch lies on the device with the same sub and half indices and a patch index one above or one below, cyclically. `elem_row`: a permutation of the rows; of each device's rows, those in positions k * 16 to (k + 1) * 16 - 1 belong to patches of the device with index k along patch+sub+half.
All inputs are finite; a program needn't handle non-finite values.
Results may differ from a plain program's by a relative error of at most 0.0003.
Values may be sent and summed in bfloat16 or wider, within the bound.
A program may use at most 64 MiB of HBM per device.

v0:
```python
import jax
import jax.numpy as jnp
from jax import lax
from jax.sharding import PartitionSpec as P

ITERS = 2


step_size = 1.0
norm_scale = 16.0
penalty_value = 8.0
penalty_slope = 4.0


def passed_along(array, axis, by):
    peers = lax.axis_size(axis)
    return lax.ppermute(array, axis, [(i, (i + by) % peers) for i in range(peers)])


def second_rows(field):
    padded = jnp.pad(field, [(0, 0)] * (field.ndim - 2) + [(1, 1), (0, 0)])
    return padded[..., :-2, :] - 2.0 * field + padded[..., 2:, :]


def second_cols(field):
    padded = jnp.pad(field, [(0, 0)] * (field.ndim - 1) + [(1, 1)])
    return padded[..., :-2] - 2.0 * field + padded[..., 2:]


def forward_rows(field):
    zeros = jnp.zeros_like(field[..., :1, :])
    return jnp.concatenate([field[..., 1:, :], zeros], axis=-2) - field


def backward_rows(field):
    zeros = jnp.zeros_like(field[..., :1, :])
    return jnp.concatenate([zeros, field[..., :-1, :]], axis=-2) - field


def forward_cols(field):
    zeros = jnp.zeros_like(field[..., :1])
    return jnp.concatenate([field[..., 1:], zeros], axis=-1) - field


def backward_cols(field):
    zeros = jnp.zeros_like(field[..., :1])
    return jnp.concatenate([zeros, field[..., :-1]], axis=-1) - field


def stiffness(field, live, thickness, foundation):
    bend_rows = thickness * live * second_rows(field)
    bend_cols = thickness * second_cols(field)
    return live * (foundation * field + second_rows(bend_rows) + second_cols(bend_cols))


def geometric(field, live, stress):
    along_rows = forward_rows(field)
    along_cols = forward_cols(field)
    nuu = stress[:, :, 0, :]
    nvv = stress[:, :, 1, :]
    nuv = stress[:, :, 2, :]
    total = backward_rows(nuu * along_rows + nuv * along_cols) + backward_cols(
        nvv * along_cols + nuv * along_rows
    )
    return live * total


def edges(field, lengths):

    def row_pick(index):
        where_rows = jnp.broadcast_to(
            index[None, :, None, None], (field.shape[0], field.shape[1], 1, field.shape[3])
        )
        return jnp.take_along_axis(field, where_rows, axis=2)[:, :, 0, :]

    top = jnp.stack([row_pick(lengths - 2), row_pick(lengths - 1)], axis=2)
    bottom = field[:, :, 0:2, :]
    return (top, bottom)


def interface(field, lengths, top, bottom, partner_top, partner_bottom):
    jump_top = top[:, :, 1, :] - partner_bottom[:, :, 0, :]
    slope_top = (
        top[:, :, 1, :]
        - top[:, :, 0, :]
        - (partner_bottom[:, :, 1, :] - partner_bottom[:, :, 0, :])
    )
    jump_bottom = partner_top[:, :, 1, :] - bottom[:, :, 0, :]
    slope_bottom = (
        partner_top[:, :, 1, :]
        - partner_top[:, :, 0, :]
        - (bottom[:, :, 1, :] - bottom[:, :, 0, :])
    )
    rows = jnp.arange(field.shape[2], dtype=jnp.int32)[None, :, None]
    last = lengths[:, None, None] - 1
    added = jnp.where(
        rows == last, (penalty_value * jump_top + penalty_slope * slope_top)[:, :, None, :], 0.0
    )
    added = added + jnp.where(rows == last - 1, (-penalty_slope * slope_top)[:, :, None, :], 0.0)
    added = added + jnp.where(
        rows == 0, (-penalty_value * jump_bottom + penalty_slope * slope_bottom)[:, :, None, :], 0.0
    )
    added = added + jnp.where(rows == 1, (-penalty_slope * slope_bottom)[:, :, None, :], 0.0)
    return added


def products(field, kfield, gfield):
    return jnp.stack(
        [
            jnp.sum(field[0] * kfield[0]),
            jnp.sum(field[0] * kfield[1]),
            jnp.sum(field[1] * kfield[1]),
            jnp.sum(field[0] * gfield[0]),
            jnp.sum(field[0] * gfield[1]),
            jnp.sum(field[1] * gfield[1]),
        ]
    )


def advance(field, kfield, gfield, totals, precond, cells):
    first_a = totals[0]
    cross_k = totals[1]
    second_a = totals[2]
    first_g = totals[3]
    cross_g = totals[4]
    second_g = totals[5]
    ratio = cross_k / first_a
    other = field[1] - ratio * field[0]
    other_k = kfield[1] - ratio * kfield[0]
    other_g = gfield[1] - ratio * gfield[0]
    other_a = second_a - ratio * cross_k
    other_q = second_g - 2.0 * ratio * cross_g + ratio * ratio * first_g
    first_mu = first_g / first_a
    other_mu = other_q / other_a
    new_first = (field[0] + step_size * precond * (gfield[0] - first_mu * kfield[0])) * jnp.sqrt(
        norm_scale * cells / first_a
    )
    new_other = (other + step_size * precond * (other_g - other_mu * other_k)) * jnp.sqrt(
        norm_scale * cells / other_a
    )
    return jnp.stack([new_first, new_other])


def choose(candidates, wanted, labels):
    match = labels[None, :] == wanted[:, None]
    return jnp.sum(jnp.where(match[None, :, :, None, None], candidates[:, None], 0.0), axis=2)


def per_device(vectors, prestress, thickness, foundation, patch_rows, matched, elem_row):
    owners = lax.axis_size("patch")
    inner = lax.axis_size(("sub", "half"))
    slots = patch_rows.shape[0]
    rows_dev = thickness.shape[0]
    prows = rows_dev // slots
    ncol = thickness.shape[1]
    per_peer = rows_dev // (owners * inner)
    blocks = prestress.reshape(owners, inner, per_peer, 3, ncol)
    targets = (elem_row % rows_dev).reshape(owners, inner, per_peer)
    arrived, arrived_rows = (
        lax.all_to_all(
            lax.all_to_all(blocks, "patch", split_axis=0, concat_axis=0, tiled=True),
            ("sub", "half"),
            split_axis=1,
            concat_axis=1,
            tiled=True,
        ),
        lax.all_to_all(
            lax.all_to_all(targets, "patch", split_axis=0, concat_axis=0, tiled=True),
            ("sub", "half"),
            split_axis=1,
            concat_axis=1,
            tiled=True,
        ),
    )
    placed = (
        jnp.zeros((rows_dev, 3, ncol), jnp.bfloat16)
        .at[arrived_rows.reshape(-1)]
        .set(arrived.reshape(-1, 3, ncol))
    )
    stress = placed.astype(jnp.float32).reshape(slots, prows, 3, ncol)
    rows = jnp.arange(prows, dtype=jnp.int32)[None, :]
    live = (rows < patch_rows[:, None]).astype(jnp.float32)[:, :, None]
    thick = thickness.reshape(slots, prows, ncol)
    support = foundation.reshape(slots, prows, ncol)
    precond = live / (support + 12.0 * thick)
    own_ids = lax.axis_index(("patch", "sub", "half")) * slots + jnp.arange(slots, dtype=jnp.int32)
    labels = jnp.stack([own_ids, matched])
    field = vectors.reshape(2, slots, prows, ncol) * live
    cells = jnp.float32(owners * inner * rows_dev * ncol)
    for step in range(ITERS):
        top, bottom = edges(field, patch_rows)
        strips = jnp.stack([top, bottom])
        below = passed_along((strips, labels), "patch", 1)
        above = passed_along((strips, labels), "patch", -1)
        got_strips = jnp.stack([below[0], above[0]])
        got_labels = jnp.stack([below[1], above[1]])
        count = got_strips.shape[0] * slots
        cand_top = jnp.moveaxis(got_strips[:, 0], 0, 1).reshape(2, count, 2, ncol)
        cand_bottom = jnp.moveaxis(got_strips[:, 1], 0, 1).reshape(2, count, 2, ncol)
        cand_ids = got_labels[:, 0].reshape(-1)
        cand_next = got_labels[:, 1].reshape(-1)
        partner_bottom = choose(cand_bottom, matched, cand_ids)
        partner_top = choose(cand_top, own_ids, cand_next)
        kfield = stiffness(field, live, thick, support) + interface(
            field, patch_rows, top, bottom, partner_top, partner_bottom
        )
        gfield = geometric(field, live, stress)
        totals = lax.psum(products(field, kfield, gfield), ("patch", "sub", "half"))
        field = advance(field, kfield, gfield, totals, precond, cells)
    return field.reshape(2, rows_dev, ncol)


def solution(mesh):
    in_specs = (
        P(None, ("groups", "patch", "sub", "half"), None),
        P(("groups", "patch", "sub", "half"), None, None),
        P(("groups", "patch", "sub", "half"), None),
        P(("groups", "patch", "sub", "half"), None),
        P(("groups", "patch", "sub", "half")),
        P(("groups", "patch", "sub", "half")),
        P(("groups", "patch", "sub", "half")),
    )
    out_specs = P(None, ("groups", "patch", "sub", "half"), None)
    return jax.shard_map(
        per_device, mesh=mesh, in_specs=in_specs, out_specs=out_specs, check_vma=False
    )
```

profile of v0, /device:TPU:0, one launch (start us, length us, event | category | flops | bytes accessed | tf_op | source)
XLA Modules:
  0.0 211.1 jit_solution(15988298672852159609)
XLA Ops:
  1.1 1.1 broadcast_multiply_fusion
  2.2 12.3 %gather_fusion = f32[1024]{0:T(1024)S(1)} fusion(f32[2,2,128,256]{3,2,1,0:T(8,128)S(1)} %broadcast_multiply_fusion, s32[1024]{0:T(1024)S(1)} %bitcast.210), kind=kCustom, calls=%fused_computation.clone | custom fusion | bytes 24576 | tf_op jit(solution)/shard_map/jit(take_along_axis)/gather | solution.py:74
  14.6 12.3 %gather_fusion.1 = f32[1024]{0:T(1024)S(1)} fusion(f32[2,2,128,256]{3,2,1,0:T(8,128)S(1)} %broadcast_multiply_fusion, s32[1024]{0:T(1024)S(1)} %bitcast.212), kind=kCustom, calls=%fused_computation.1.clone | custom fusion | bytes 24576 | tf_op jit(solution)/shard_map/jit(take_along_axis)/gather | solution.py:74
  27.1 3.1 %collective-permute-start.2 = (f32[2,2,2,2,256]{4,3,2,1,0:T(2,128)S(1)}, f32[2,2,2,2,256]{4,3,2,1,0:T(2,128)S(1)}, u32[]{:S(2)}, u32[]{:S(2)}) collective-permute-start(f32[2,2,2,2,256]{4,3,2,1,0:T(2,128)S(1)} %pad_maximum_fusion.4), channel_id=1, source_target_pairs={{0,4},{4,8},{8,12},{12,0},{1,5},{5,9},{9,13},{13,1},{2,6},{6,10},{... | collective-permute-start | bytes 49160 | tf_op jit(solution)/shard_map/ppermute | solution.py:17
  30.1 2.1 collective-permute-start.3
  33.0 3.8 %collective-permute-start.1 = (s32[2,2]{1,0:T(2,128)S(1)}, s32[2,2]{1,0:T(2,128)S(1)}, u32[]{:S(2)}, u32[]{:S(2)}) collective-permute-start(s32[2,2]{1,0:T(2,128)S(1)} %pad_add_fusion.4), channel_id=1, source_target_pairs={{0,12},{4,0},{8,4},{12,8},{1,13},{5,1},{9,5},{13,9},{2,14},{6,2},{... | collective-permute-start | bytes 56 | tf_op jit(solution)/shard_map/ppermute | solution.py:17
  37.5 3.2 %all-to-all-start = ((s32[4,4,16]{2,1,0:T(4,128)}), s32[4,4,16]{2,1,0:T(4,128)S(1)}, u32[]{:S(2)}, u32[]{:S(2)}) async-start(s32[4,4,16]{2,1,0:T(4,128)} %reshape.291), calls=%async_computation | async-start | bytes 16384 | tf_op jit(solution)/shard_map/all_to_all | solution.py:168
  43.8 2.4 %all-to-all-done = s32[4,4,16]{2,1,0:T(4,128)S(1)} async-done(((s32[4,4,16]{2,1,0:T(4,128)}), s32[4,4,16]{2,1,0:T(4,128)S(1)}, u32[]{:S(2)}, u32[]{:S(2)}) %all-to-all-start) | async-done | bytes 1056 | tf_op jit(solution)/shard_map/all_to_all | solution.py:168
  46.9 3.2 %all-to-all-start.1 = ((s32[4,4,16]{2,0,1:T(4,128)}), s32[4,4,16]{2,0,1:T(4,128)S(1)}, u32[]{:S(2)}, u32[]{:S(2)}) async-start(s32[4,4,16]{2,0,1:T(4,128)} %copy.28), calls=%async_computation.1 | async-start | bytes 16384 | tf_op jit(solution)/shard_map/all_to_all | solution.py:167
  50.2 3.7 %all-to-all-done.1 = s32[4,4,16]{2,0,1:T(4,128)S(1)} async-done(((s32[4,4,16]{2,0,1:T(4,128)}), s32[4,4,16]{2,0,1:T(4,128)S(1)}, u32[]{:S(2)}, u32[]{:S(2)}) %all-to-all-start.1) | async-done | bytes 1056 | tf_op jit(solution)/shard_map/all_to_all | solution.py:167
  53.9 3.5 %all-to-all-start.2 = ((bf16[4,4,16,3,256]{4,2,1,3,0:T(8,128)(2,1)}), bf16[4,4,16,3,256]{4,2,1,3,0:T(8,128)(2,1)S(1)}, u32[]{:S(2)}, u32[]{:S(2)}) async-start(bf16[4,4,16,3,256]{4,2,1,3,0:T(8,128)(2,1)} %copy.30), calls=%async_computation.2 | async-start | bytes 786432 | tf_op jit(solution)/shard_map/all_to_all | solution.py:161
  57.8 11.4 %all-to-all-done.2 = bf16[4,4,16,3,256]{4,2,1,3,0:T(8,128)(2,1)S(1)} async-done(((bf16[4,4,16,3,256]{4,2,1,3,0:T(8,128)(2,1)}), bf16[4,4,16,3,256]{4,2,1,3,0:T(8,128)(2,1)S(1)}, u32[]{:S(2)}, u32[]{:S(2)}) %all-to-all-start.2) | async-done | bytes 393248 | tf_op jit(solution)/shard_map/all_to_all | solution.py:161
  70.0 3.5 %all-to-all-start.3 = ((bf16[4,4,16,3,256]{4,2,0,3,1:T(8,128)(2,1)}), bf16[4,4,16,3,256]{4,2,0,3,1:T(8,128)(2,1)S(1)}, u32[]{:S(2)}, u32[]{:S(2)}) async-start(bf16[4,4,16,3,256]{4,2,0,3,1:T(8,128)(2,1)} %copy.31), calls=%async_computation.3 | async-start | bytes 786432 | tf_op jit(solution)/shard_map/all_to_all | solution.py:160
  73.6 7.3 %all-to-all-done.3 = bf16[4,4,16,3,256]{4,2,0,3,1:T(8,128)(2,1)S(1)} async-done(((bf16[4,4,16,3,256]{4,2,0,3,1:T(8,128)(2,1)}), bf16[4,4,16,3,256]{4,2,0,3,1:T(8,128)(2,1)S(1)}, u32[]{:S(2)}, u32[]{:S(2)}) %all-to-all-start.3) | async-done | bytes 393248 | tf_op jit(solution)/shard_map/all_to_all | solution.py:160
  81.4 7.0 %scatter_fusion = bf16[256,3,256]{2,1,0:T(4,128)(2,1)S(1)} fusion(bf16[256,3,256]{2,1,0:T(4,128)(2,1)S(1)} %broadcast_in_dim.225, s32[256]{0:T(256)S(1)} %bitcast.260, bf16[256,3,256]{2,1,0:T(4,128)(2,1)S(1)} %copy.33), kind=kCustom, calls=%fused_computation.4 | custom fusion | bytes 1180672 | tf_op jit(solution)/shard_map/scatter | solution.py:178
  89.1 1.2 copy-done.7
  93.0 3.8 %stack.135 = f32[6]{0:T(128)S(1)} concatenate(f32[1]{0:T(128)} %bitcast.30, f32[1]{0:T(128)} %bitcast.32, f32[1]{0:T(128)} %bitcast.34, f32[1]{0:T(128)} %bitcast.36, f32[1]{0:T(128)} %bitcast.38, f32[1]{0:T(128)} %bitcast.39), dimensions={0} | concatenate | bytes 48 | tf_op jit(solution)/shard_map/stack | solution.py:108
  96.8 30.2 %psum.14 = f32[6]{0:T(128)S(1)} all-reduce(f32[6]{0:T(128)S(1)} %stack.135), channel_id=1, replica_groups=mesh['groups'=2,'patch'=4,'sub'=2,'half'=2] {'patch','sub','half'}, use_global_device_ids=true, to_apply=%region_9.11 | all-reduce | flops 6 | bytes 48 | tf_op jit(solution)/shard_map/psum | solution.py:208
  136.7 12.3 %gather_fusion.3 = f32[1024]{0:T(1024)S(1)} fusion(f32[2,2,128,256]{3,2,1,0:T(8,128)S(1)} %get-tuple-element.46, s32[1024]{0:T(1024)S(1)} %bitcast.213), kind=kCustom, calls=%fused_computation.3.clone | custom fusion | bytes 24576 | tf_op jit(solution)/shard_map/jit(take_along_axis)/gather | solution.py:74
  149.1 12.3 %gather_fusion.2 = f32[1024]{0:T(1024)S(1)} fusion(f32[2,2,128,256]{3,2,1,0:T(8,128)S(1)} %get-tuple-element.46, s32[1024]{0:T(1024)S(1)} %bitcast.211), kind=kCustom, calls=%fused_computation.2.clone | custom fusion | bytes 24576 | tf_op jit(solution)/shard_map/jit(take_along_axis)/gather | solution.py:74
  161.6 3.8 %collective-permute-start.5 = (f32[2,2,2,2,256]{4,3,2,1,0:T(2,128)S(1)}, f32[2,2,2,2,256]{4,3,2,1,0:T(2,128)S(1)}, u32[]{:S(2)}, u32[]{:S(2)}) collective-permute-start(f32[2,2,2,2,256]{4,3,2,1,0:T(2,128)S(1)} %pad_maximum_fusion.5), channel_id=1, source_target_pairs={{0,12},{4,0},{8,4},{12,8},{1,13},{5,1},{9,5},{13,9},{2,14},{6,2},{... | collective-permute-start | bytes 49160 | tf_op jit(solution)/shard_map/ppermute | solution.py:17
  166.1 1.1 collective-permute-done.4
  169.5 3.8 %stack.150 = f32[6]{0:T(128)S(1)} concatenate(f32[1]{0:T(128)} %bitcast.59, f32[1]{0:T(128)} %bitcast.61, f32[1]{0:T(128)} %bitcast.62, f32[1]{0:T(128)} %bitcast.64, f32[1]{0:T(128)} %bitcast.66, f32[1]{0:T(128)} %bitcast.67), dimensions={0} | concatenate | bytes 48 | tf_op jit(solution)/shard_map/stack | solution.py:108
  173.4 29.5 %psum.15 = f32[6]{0:T(128)S(1)} all-reduce(f32[6]{0:T(128)S(1)} %stack.150), channel_id=1, replica_groups=mesh['groups'=2,'patch'=4,'sub'=2,'half'=2] {'patch','sub','half'}, use_global_device_ids=true, to_apply=%region_18.20 | all-reduce | flops 6 | bytes 48 | tf_op jit(solution)/shard_map/psum | solution.py:208
  (130 shorter events, 19.5 us)
Async XLA Ops:
  0.0 0.7 copy-start.12
  27.1 30.4 %collective-permute-start.2 = (f32[2,2,2,2,256]{4,3,2,1,0:T(2,128)S(1)}, f32[2,2,2,2,256]{4,3,2,1,0:T(2,128)S(1)}, u32[]{:S(2)}, u32[]{:S(2)}) collective-permute-start(f32[2,2,2,2,256]{4,3,2,1,0:T(2,128)S(1)} %pad_maximum_fusion.4), channel_id=1, source_target_pairs={{0,4},{4,8},{8,12},{12,0},{1,5},{5,9},{9,13},{13,1},{2,6},{6,10},{... | collective-permute-start | bytes 49160 | tf_op jit(solution)/shard_map/ppermute | solution.py:17
  30.1 27.3 %collective-permute-start.3 = (f32[2,2,2,2,256]{4,3,2,1,0:T(2,128)S(1)}, f32[2,2,2,2,256]{4,3,2,1,0:T(2,128)S(1)}, u32[]{:S(2)}, u32[]{:S(2)}) collective-permute-start(f32[2,2,2,2,256]{4,3,2,1,0:T(2,128)S(1)} %pad_maximum_fusion.4), channel_id=1, source_target_pairs={{0,12},{4,0},{8,4},{12,8},{1,13},{5,1},{9,5},{13,9},{2,14},{6,2},{... | collective-permute-start | bytes 49160 | tf_op jit(solution)/shard_map/ppermute | solution.py:17
  32.2 0.7 copy-start.13
  32.9 3.9 %copy-start.11 = (s32[256]{0:T(256)S(1)}, s32[256]{0:T(256)}, u32[]{:S(2)}) copy-start(s32[256]{0:T(256)} %param.15) | copy-start | bytes 3076
  32.9 10.7 %collective-permute-start = (s32[2,2]{1,0:T(2,128)S(1)}, s32[2,2]{1,0:T(2,128)S(1)}, u32[]{:S(2)}, u32[]{:S(2)}) collective-permute-start(s32[2,2]{1,0:T(2,128)S(1)} %pad_add_fusion.4), channel_id=1, source_target_pairs={{0,4},{4,8},{8,12},{12,0},{1,5},{5,9},{9,13},{13,1},{2,6},{6,10},{... | collective-permute-start | bytes 56 | tf_op jit(solution)/shard_map/ppermute | solution.py:17
  33.0 10.6 %collective-permute-start.1 = (s32[2,2]{1,0:T(2,128)S(1)}, s32[2,2]{1,0:T(2,128)S(1)}, u32[]{:S(2)}, u32[]{:S(2)}) collective-permute-start(s32[2,2]{1,0:T(2,128)S(1)} %pad_add_fusion.4), channel_id=1, source_target_pairs={{0,12},{4,0},{8,4},{12,8},{1,13},{5,1},{9,5},{13,9},{2,14},{6,2},{... | collective-permute-start | bytes 56 | tf_op jit(solution)/shard_map/ppermute | solution.py:17
  37.5 8.8 %all-to-all-start = ((s32[4,4,16]{2,1,0:T(4,128)}), s32[4,4,16]{2,1,0:T(4,128)S(1)}, u32[]{:S(2)}, u32[]{:S(2)}) async-start(s32[4,4,16]{2,1,0:T(4,128)} %reshape.291), calls=%async_computation | async-start | bytes 16384 | tf_op jit(solution)/shard_map/all_to_all | solution.py:168
  40.8 1.1 copy-start
  41.8 1.0 copy-start.10
  46.9 7.0 %all-to-all-start.1 = ((s32[4,4,16]{2,0,1:T(4,128)}), s32[4,4,16]{2,0,1:T(4,128)S(1)}, u32[]{:S(2)}, u32[]{:S(2)}) async-start(s32[4,4,16]{2,0,1:T(4,128)} %copy.28), calls=%async_computation.1 | async-start | bytes 16384 | tf_op jit(solution)/shard_map/all_to_all | solution.py:167
  53.9 15.4 %all-to-all-start.2 = ((bf16[4,4,16,3,256]{4,2,1,3,0:T(8,128)(2,1)}), bf16[4,4,16,3,256]{4,2,1,3,0:T(8,128)(2,1)S(1)}, u32[]{:S(2)}, u32[]{:S(2)}) async-start(bf16[4,4,16,3,256]{4,2,1,3,0:T(8,128)(2,1)} %copy.30), calls=%async_computation.2 | async-start | bytes 786432 | tf_op jit(solution)/shard_map/all_to_all | solution.py:161
  70.0 10.9 %all-to-all-start.3 = ((bf16[4,4,16,3,256]{4,2,0,3,1:T(8,128)(2,1)}), bf16[4,4,16,3,256]{4,2,0,3,1:T(8,128)(2,1)S(1)}, u32[]{:S(2)}, u32[]{:S(2)}) async-start(bf16[4,4,16,3,256]{4,2,0,3,1:T(8,128)(2,1)} %copy.31), calls=%async_computation.3 | async-start | bytes 786432 | tf_op jit(solution)/shard_map/all_to_all | solution.py:160
  89.0 1.2 copy-start.7
  89.0 1.6 copy-start.2
  89.0 1.6 copy-start.4
  90.2 0.9 copy-start.1
  90.2 1.1 copy-start.6
  135.5 1.0 copy-start.3
  135.5 1.0 copy-start.5
  161.6 5.6 %collective-permute-start.4 = (f32[2,2,2,2,256]{4,3,2,1,0:T(2,128)S(1)}, f32[2,2,2,2,256]{4,3,2,1,0:T(2,128)S(1)}, u32[]{:S(2)}, u32[]{:S(2)}) collective-permute-start(f32[2,2,2,2,256]{4,3,2,1,0:T(2,128)S(1)} %pad_maximum_fusion.5), channel_id=1, source_target_pairs={{0,4},{4,8},{8,12},{12,0},{1,5},{5,9},{9,13},{13,1},{2,6},{6,10},{... | collective-permute-start | bytes 49160 | tf_op jit(solution)/shard_map/ppermute | solution.py:17
  161.6 5.5 %collective-permute-start.5 = (f32[2,2,2,2,256]{4,3,2,1,0:T(2,128)S(1)}, f32[2,2,2,2,256]{4,3,2,1,0:T(2,128)S(1)}, u32[]{:S(2)}, u32[]{:S(2)}) collective-permute-start(f32[2,2,2,2,256]{4,3,2,1,0:T(2,128)S(1)} %pad_maximum_fusion.5), channel_id=1, source_target_pairs={{0,12},{4,0},{8,4},{12,8},{1,13},{5,1},{9,5},{13,9},{2,14},{6,2},{... | collective-permute-start | bytes 49160 | tf_op jit(solution)/shard_map/ppermute | solution.py:17
  167.6 1.0 copy-start.8
  167.7 1.0 copy-start.9
where the time goes:
time: 212 us; the launch traced here: 211 us
  local copies, waits for them, and re-layouts  75.2 us (35%)
  blocking collectives  59.7 us (28%)
  starting transfers between devices  26.3 us (12%)
  waiting for transfers between devices  26 us (12%)
  between operations  13.6 us (6%)
  other arithmetic  10.3 us (5%)
    psum x2, blocking collectives, per_device(): totals = lax.psum(products(field, kfield, gfield), ('patch', 'sub', 'half'))  59.7 us
    gather x4, local copies, waits for them, and re-layouts, row_pick(): return jnp.take_along_axis(field, where_rows, axis=2)[:, :, 0, :]  49.2 us
    ppermute x6, starting transfers between devices, passed_along(): lax.ppermute(array, axis, [(i, (i + by) % peers) for i in range(peers)])  12.9 us
    all_to_all x1, waiting for transfers between devices, per_device(): lax.all_to_all(blocks, 'patch', split_axis=0, concat_axis=0, tiled=True)  11.4 us
    another operation x2, local copies, waits for them, and re-layouts, products(): jnp.stack([jnp.sum(field[0] * kfield[0]), jnp.sum(field[0] * kfield[1]),...  7.63 us
    all_to_all x1, waiting for transfers between devices, per_device(): lax.all_to_all(lax.all_to_all(blocks, 'patch', split_axis=0, concat_axis=...  7.33 us
    scatter x1, local copies, waits for them, and re-layouts, per_device(): placed = jnp.zeros((rows_dev, 3, ncol), jnp.bfloat16).at[arrived_rows.res...  6.97 us
    unnamed x40, local copies, waits for them, and re-layouts  4.77 us
  transfers between devices with their start and end apart: 10, of which 5 were waited for; matrix products, arithmetic and copies ran while one was open for 2% of the time, Pallas kernels for 0%

commit v1 on v0

v1 whole, which is shorter than its diff:
```python
import jax
import jax.numpy as jnp
from jax import lax
from jax.experimental import pallas as pl
from jax.experimental.pallas import tpu as pltpu
from jax.sharding import PartitionSpec as P

step_size = 1.0
norm_scale = 16.0
penalty_value = 8.0
penalty_slope = 4.0

MESH = pl.DeviceIdType.MESH
PAD = 8
LANES = 128
CHUNK = 32


def body(
    vec, pre, thick_in, found_in, lengths, matched, elem, out,
    x, thick, found, prec, stress, mrow, frow, kpart, gpart, kf, gf,
    arrived, ids, strips, got, edge, sums, coef,
    load_sem, own_sem, data_send, data_recv, ids_send, ids_recv,
    strip_send, strip_recv, sum_send, sum_recv,
):
    owners, subs, halves = (lax.axis_size(a) for a in ("patch", "sub", "half"))
    n = owners * subs * halves
    pi, si, hi = (lax.axis_index(a) for a in ("patch", "sub", "half"))
    me = (pi * subs + si) * halves + hi
    slots = x.shape[1]
    prows = x.shape[2] - 2 * PAD
    ncol = x.shape[3]
    rows_dev = slots * prows
    per_peer = rows_dev // n
    chunk = CHUNK
    per_slot = prows // chunk
    steps = slots * per_slot

    def peer(d):
        k = lax.rem(me + d, n)
        where = {
            "patch": lax.div(k, subs * halves),
            "sub": lax.rem(lax.div(k, halves), subs),
            "half": lax.rem(k, halves),
        }
        return k, where

    barrier = pltpu.get_barrier_semaphore()

    @pl.loop(1, n)
    def _(d):
        _, where = peer(d)
        pl.semaphore_signal(barrier, inc=1, device_id=where, device_id_type=MESH)

    loads = []
    for v in range(2):
        for s in range(slots):
            loads.append(
                pltpu.make_async_copy(
                    vec.at[v, pl.ds(s * prows, prows)],
                    x.at[v, s, pl.ds(PAD, prows)],
                    load_sem.at[v * slots + s],
                )
            )
    load_thick = pltpu.make_async_copy(thick_in, thick, load_sem.at[2 * slots])
    load_found = pltpu.make_async_copy(found_in, found, load_sem.at[2 * slots + 1])
    own_data = pltpu.make_async_copy(pre.at[:, me], arrived.at[:, me], own_sem.at[0])
    own_ids = pltpu.make_async_copy(elem, ids.at[me], own_sem.at[1])
    for copy in loads + [load_thick, load_found, own_data, own_ids]:
        copy.start()

    zero_pad = jnp.zeros((PAD, ncol), jnp.float32)
    for v in range(2):
        for s in range(slots):
            for ref in (x, mrow, frow):
                ref[v, s, 0:PAD, :] = zero_pad
                ref[v, s, PAD + prows : 2 * PAD + prows, :] = zero_pad
    for copy in loads:
        copy.wait()

    def fill_strip(which, row_of):
        for s in range(slots):
            length = jnp.maximum(lengths[s], 2)
            for v in range(2):
                base = (s * 2 + v) * 4
                for r, at in enumerate((length - 2, length - 1, 0, 1)):
                    strips[which, base + r : base + r + 1, :] = row_of(s, v, at)

    rows_strip = slots * 2 * 4
    fill_strip(0, lambda s, v, at: x[v, s, pl.ds(PAD + at, 1), :])
    for s in range(slots):
        strips[0, rows_strip + s : rows_strip + s + 1, :] = jnp.full(
            (1, ncol), matched[s], jnp.int32
        ).astype(jnp.float32)

    pl.semaphore_wait(barrier, n - 1)

    def strip_copies(which, rows):
        copies = []
        for side, by in ((0, 1), (1, owners - 1)):
            copies.append(
                pltpu.make_async_remote_copy(
                    src_ref=strips.at[which, pl.ds(0, rows)],
                    dst_ref=got.at[which, side, pl.ds(0, rows)],
                    send_sem=strip_send.at[which * 2 + side],
                    recv_sem=strip_recv.at[which * 2 + side],
                    device_id={"patch": lax.rem(pi + by, owners)},
                    device_id_type=MESH,
                )
            )
        return copies

    first_strips = strip_copies(0, strips.shape[1])
    for copy in first_strips:
        copy.start()

    @pl.loop(1, n)
    def _(d):
        k, where = peer(d)
        pltpu.make_async_remote_copy(
            src_ref=elem, dst_ref=ids.at[me], send_sem=ids_send.at[0],
            recv_sem=ids_recv.at[0], device_id=where, device_id_type=MESH,
        ).start()
        pltpu.make_async_remote_copy(
            src_ref=pre.at[:, k], dst_ref=arrived.at[:, me], send_sem=data_send.at[0],
            recv_sem=data_recv.at[0], device_id=where, device_id_type=MESH,
        ).start()

    def all_ids():
        part = ids.at[pl.ds(0, n - 1)]
        return pltpu.make_async_remote_copy(
            src_ref=part, dst_ref=part, send_sem=ids_send.at[0], recv_sem=ids_recv.at[0],
            device_id={"patch": pi}, device_id_type=MESH,
        )

    def all_data():
        part = arrived.at[:, pl.ds(0, n - 1)]
        return pltpu.make_async_remote_copy(
            src_ref=part, dst_ref=part, send_sem=data_send.at[0], recv_sem=data_recv.at[0],
            device_id={"patch": pi}, device_id_type=MESH,
        )

    lane = lax.broadcasted_iota(jnp.int32, (chunk, ncol), 1)
    first_lane = lane == 0
    last_lane = lane == ncol - 1
    sub_row = lax.broadcasted_iota(jnp.int32, (chunk, ncol), 0)

    def before(w):
        return jnp.where(first_lane, 0.0, pltpu.roll(w, 1, 1))

    def after(w):
        return jnp.where(last_lane, 0.0, pltpu.roll(w, ncol - 1, 1))

    def place(i):
        s = lax.div(i, per_slot)
        r0 = pl.multiple_of(lax.rem(i, per_slot) * chunk, chunk)
        full = pl.multiple_of(i * chunk, chunk)
        return s, r0, pl.ds(full, chunk), r0 + sub_row, lengths[s]

    def shifted(ref, v, s, r0, by):
        window = ref.at[v, s, pl.ds(r0, chunk + 2 * PAD)]
        return window[PAD + by : PAD + by + chunk, :]

    load_thick.wait()
    load_found.wait()

    @pl.loop(0, steps)
    def _(i):
        s, r0, full, row, length = place(i)
        live = row < length
        for v in range(2):
            at = pl.ds(r0 + PAD, chunk)
            x[v, s, at, :] = jnp.where(live, x[v, s, at, :], 0.0)
        prec[full, :] = jnp.where(live, 1.0, 0.0) / (found[full, :] + 12.0 * thick[full, :])

    def stiff_first(i):
        s, r0, full, row, length = place(i)
        th = thick[full, :]
        fo = found[full, :]
        live_th = jnp.where(row < length, th, 0.0)
        for v in range(2):
            w = shifted(x, v, s, r0, 0)
            mrow[v, s, pl.ds(r0 + PAD, chunk), :] = live_th * (
                shifted(x, v, s, r0, -1) - 2.0 * w + shifted(x, v, s, r0, 1)
            )
            bend = th * (before(w) - 2.0 * w + after(w))
            kpart[v, full, :] = fo * w + (before(bend) - 2.0 * bend + after(bend))

    def geo_first(i):
        s, r0, full, row, length = place(i)
        nuu = stress[0, full, :]
        nvv = stress[1, full, :]
        nuv = stress[2, full, :]
        for v in range(2):
            w = shifted(x, v, s, r0, 0)
            along_rows = shifted(x, v, s, r0, 1) - w
            along_cols = after(w) - w
            frow[v, s, pl.ds(r0 + PAD, chunk), :] = nuu * along_rows + nuv * along_cols
            cols = nvv * along_cols + nuv * along_rows
            gpart[v, full, :] = before(cols) - cols

    def fold(value):
        total = value[0:8]
        for j in range(8, chunk, 8):
            total = total + value[j : j + 8]
        return total

    def stiff_second(i, acc):
        s, r0, full, row, length = place(i)
        ks = []
        for v in range(2):
            m = shifted(mrow, v, s, r0, 0)
            bent = shifted(mrow, v, s, r0, -1) - 2.0 * m + shifted(mrow, v, s, r0, 1)
            k = jnp.where(row < length, kpart[v, full, :] + bent, 0.0)

            def line(r):
                return edge[s, v, r : r + 1, :]

            joint = jnp.where(row == length - 1, line(0), 0.0)
            joint = jnp.where(row == length - 2, line(1), joint)
            joint = jnp.where(row == 0, line(2), joint)
            joint = jnp.where(row == 1, line(3), joint)
            k = k + joint
            kf[v, full, :] = k
            ks.append(k)
        x0 = shifted(x, 0, s, r0, 0)
        x1 = shifted(x, 1, s, r0, 0)
        return (
            acc[0] + fold(x0 * ks[0]),
            acc[1] + fold(x0 * ks[1]),
            acc[2] + fold(x1 * ks[1]),
        )

    def geo_second(i, acc):
        s, r0, full, row, length = place(i)
        gs = []
        for v in range(2):
            g = shifted(frow, v, s, r0, -1) - shifted(frow, v, s, r0, 0) + gpart[v, full, :]
            g = jnp.where(row < length, g, 0.0)
            gf[v, full, :] = g
            gs.append(g)
        x0 = shifted(x, 0, s, r0, 0)
        x1 = shifted(x, 1, s, r0, 0)
        return (
            acc[0] + fold(x0 * gs[0]),
            acc[1] + fold(x0 * gs[1]),
            acc[2] + fold(x1 * gs[1]),
        )

    def chosen(which, v, s):
        wanted = jnp.full((2, ncol), matched[s], jnp.int32)
        mine = (me * slots + s).astype(jnp.float32)
        bottom = jnp.zeros((2, ncol), jnp.float32)
        top = jnp.zeros((2, ncol), jnp.float32)
        for side, by in ((0, owners - 1), (1, 1)):
            other = (lax.rem(pi + by, owners) * subs + si) * halves + hi
            for t in range(slots):
                base = (t * 2 + v) * 4
                bottom = bottom + jnp.where(
                    wanted == other * slots + t, got[which, side, base + 2 : base + 4, :], 0.0
                )
                label = got[0, side, rows_strip + t : rows_strip + t + 1, :]
                top = top + jnp.where(label == mine, got[which, side, base : base + 2, :], 0.0)
        return top, bottom

    def set_edge(s, v, partner_top, partner_bottom):
        length = jnp.maximum(lengths[s], 2)
        top0 = x[v, s, pl.ds(PAD + length - 2, 1), :]
        top1 = x[v, s, pl.ds(PAD + length - 1, 1), :]
        bot0 = x[v, s, PAD : PAD + 1, :]
        bot1 = x[v, s, PAD + 1 : PAD + 2, :]
        ptop0, ptop1 = partner_top[0:1], partner_top[1:2]
        pbot0, pbot1 = partner_bottom[0:1], partner_bottom[1:2]
        jump_top = top1 - pbot0
        slope_top = top1 - top0 - (pbot1 - pbot0)
        jump_bottom = ptop1 - bot0
        slope_bottom = ptop1 - ptop0 - (bot1 - bot0)
        edge[s, v, 0:1, :] = penalty_value * jump_top + penalty_slope * slope_top
        edge[s, v, 1:2, :] = -penalty_slope * slope_top
        edge[s, v, 2:3, :] = -penalty_value * jump_bottom + penalty_slope * slope_bottom
        edge[s, v, 3:4, :] = -penalty_slope * slope_bottom

    def sum_copy(it, where):
        return pltpu.make_async_remote_copy(
            src_ref=sums.at[it, me], dst_ref=sums.at[it, me], send_sem=sum_send.at[it],
            recv_sem=sum_recv.at[it], device_id=where, device_id_type=MESH,
        )

    def all_sums(it):
        part = sums.at[it, pl.ds(0, n - 1)]
        return pltpu.make_async_remote_copy(
            src_ref=part, dst_ref=part, send_sem=sum_send.at[it], recv_sem=sum_recv.at[it],
            device_id={"patch": pi}, device_id_type=MESH,
        )

    def send_sums(it, totals):
        spot = lax.broadcasted_iota(jnp.int32, (1, LANES), 1)
        line = jnp.zeros((1, LANES), jnp.float32)
        for t, total in enumerate(totals):
            one = jnp.sum(jnp.sum(total, axis=0, keepdims=True), axis=1, keepdims=True)
            line = jnp.where(spot == t, one, line)
        sums[it, me] = line

        @pl.loop(1, n)
        def _(d):
            _, where = peer(d)
            sum_copy(it, where).start()

    def read_sums(it):
        all_sums(it).wait_recv()
        line = jnp.sum(sums[it], axis=0)
        first_a, cross_k, second_a, first_g, cross_g, second_g = (
            line[:, t : t + 1] for t in range(6)
        )
        cells = float(n * rows_dev * ncol)
        ratio = cross_k / first_a
        other_a = second_a - ratio * cross_k
        other_q = second_g - 2.0 * ratio * cross_g + ratio * ratio * first_g
        values = (
            ratio,
            first_g / first_a,
            other_q / other_a,
            jnp.sqrt(norm_scale * cells / first_a),
            jnp.sqrt(norm_scale * cells / other_a),
        )
        for t, value in enumerate(values):
            coef[t : t + 1, :] = jnp.broadcast_to(value, (1, ncol))

    def stepped(x0, x1, pk0, pk1, pg0, pg1):
        ratio, mu1, mu2, scale0, scale1 = (coef[t : t + 1, :] for t in range(5))
        new0 = (x0 + step_size * (pg0 - mu1 * pk0)) * scale0
        new1 = (
            (x1 - ratio * x0) + step_size * ((pg1 - ratio * pg0) - mu2 * (pk1 - ratio * pk0))
        ) * scale1
        return new0, new1

    def advanced(i):
        s, r0, full, row, length = place(i)
        ratio, mu1, mu2, scale0, scale1 = (coef[t : t + 1, :] for t in range(5))
        p = step_size * prec[full, :]
        x0 = shifted(x, 0, s, r0, 0)
        k0 = kf[0, full, :]
        g0 = gf[0, full, :]
        new0 = (x0 + p * (g0 - mu1 * k0)) * scale0
        y = shifted(x, 1, s, r0, 0) - ratio * x0
        ky = kf[1, full, :] - ratio * k0
        gy = gf[1, full, :] - ratio * g0
        new1 = (y + p * (gy - mu2 * ky)) * scale1
        return s, r0, full, new0, new1

    nothing = tuple(jnp.zeros((8, ncol), jnp.float32) for _ in range(3))

    pl.loop(0, steps)(stiff_first)
    for copy in first_strips:
        copy.wait_recv()
    for s in range(slots):
        for v in range(2):
            set_edge(s, v, *chosen(0, v, s))
    k_sums = lax.fori_loop(0, steps, stiff_second, nothing)

    def scaled_row(ref):
        def pick(s, v, at):
            spot = pl.ds(s * prows + at, 1)
            return prec[spot, :] * ref[v, spot, :]

        return pick

    fill_strip(1, scaled_row(kf))
    second_strips = strip_copies(1, rows_strip)
    for copy in second_strips:
        copy.start()

    own_ids.wait()
    all_ids().wait_recv()
    who = jnp.broadcast_to(ids[...], (n, per_peer, ncol)).reshape(rows_dev, ncol)
    wide_lane = lax.broadcasted_iota(jnp.int32, (rows_dev, ncol), 1)
    wide_row = lax.broadcasted_iota(jnp.int32, (rows_dev, ncol), 0)
    pick = wide_lane == me * per_peer + lax.rem(wide_row, per_peer)
    target = lax.rem(
        jnp.sum(jnp.where(pick, who, 0).astype(jnp.float32), axis=1, keepdims=True).astype(jnp.int32),
        rows_dev,
    )
    to = lax.broadcasted_iota(jnp.int32, (rows_dev, rows_dev), 1)
    onehot = (to == target).astype(jnp.float32).astype(jnp.bfloat16)

    own_data.wait()
    all_data().wait_recv()
    for c in range(3):
        block = arrived[c]
        if per_peer % 8:
            block = block.astype(jnp.float32).reshape(rows_dev, ncol).astype(jnp.bfloat16)
        else:
            block = block.reshape(rows_dev, ncol)
        stress[c] = lax.dot_general(
            onehot, block, (((0,), (0,)), ((), ())), preferred_element_type=jnp.float32
        )

    pl.loop(0, steps)(geo_first)
    g_sums = lax.fori_loop(0, steps, geo_second, nothing)
    send_sums(0, k_sums + g_sums)
    fill_strip(2, scaled_row(gf))
    third_strips = strip_copies(2, rows_strip)
    for copy in third_strips:
        copy.start()

    read_sums(0)

    @pl.loop(0, steps)
    def _(i):
        s, r0, full, new0, new1 = advanced(i)
        x[0, s, pl.ds(r0 + PAD, chunk), :] = new0
        x[1, s, pl.ds(r0 + PAD, chunk), :] = new1

    @pl.loop(0, steps)
    def _(i):
        stiff_first(i)
        geo_first(i)

    for copy in second_strips + third_strips:
        copy.wait_recv()
    for s in range(slots):
        parts = [[chosen(which, v, s) for v in range(2)] for which in range(3)]
        ends = []
        for end in range(2):
            ends.append(stepped(*(parts[which][v][end] for which in range(3) for v in range(2))))
        for v in range(2):
            set_edge(s, v, ends[0][v], ends[1][v])

    def second(i, acc):
        return stiff_second(i, acc[:3]) + geo_second(i, acc[3:])

    totals = lax.fori_loop(0, steps, second, nothing + nothing)
    send_sums(1, totals)
    read_sums(1)

    @pl.loop(0, steps)
    def _(i):
        s, r0, full, new0, new1 = advanced(i)
        out[0, full, :] = new0
        out[1, full, :] = new1

    for copy in first_strips + second_strips + third_strips:
        copy.wait_send()
    all_ids().wait_send()
    all_data().wait_send()
    all_sums(0).wait_send()
    all_sums(1).wait_send()


def per_device(vectors, prestress, thickness, foundation, patch_rows, matched, elem_row):
    n = lax.axis_size(("patch", "sub", "half"))
    slots = patch_rows.shape[0]
    rows_dev, ncol = thickness.shape
    prows = rows_dev // slots
    per_peer = rows_dev // n
    pre = jnp.transpose(prestress, (1, 0, 2)).reshape(3, n, per_peer, ncol)
    elem = elem_row.reshape(1, rows_dev)
    f32 = jnp.float32
    padded = pltpu.VMEM((2, slots, prows + 2 * PAD, ncol), f32)
    flat = pltpu.VMEM((rows_dev, ncol), f32)
    pair = pltpu.VMEM((2, rows_dev, ncol), f32)
    strip_rows = slots * 8 + -(-slots // 8) * 8
    anywhere = pl.BlockSpec(memory_space=pl.ANY)
    scalars = pl.BlockSpec(memory_space=pltpu.SMEM)
    dma = pltpu.SemaphoreType.DMA
    return pl.pallas_call(
        body,
        out_shape=jax.ShapeDtypeStruct((2, rows_dev, ncol), f32),
        in_specs=[anywhere] * 4 + [scalars] * 2 + [anywhere],
        out_specs=pl.BlockSpec(memory_space=pltpu.VMEM),
        scratch_shapes=[
            padded, flat, flat, flat,
            pltpu.VMEM((3, rows_dev, ncol), f32),
            padded, padded, pair, pair, pair, pair,
            pltpu.VMEM((3, n, per_peer, ncol), jnp.bfloat16),
            pltpu.VMEM((n, 1, rows_dev), jnp.int32),
            pltpu.VMEM((3, strip_rows, ncol), f32),
            pltpu.VMEM((3, 2, strip_rows, ncol), f32),
            pltpu.VMEM((slots, 2, 8, ncol), f32),
            pltpu.VMEM((2, n, 1, LANES), f32),
            pltpu.VMEM((8, ncol), f32),
            dma((2 * slots + 2,)), dma((2,)),
            dma((1,)), dma((1,)), dma((1,)), dma((1,)),
            dma((6,)), dma((6,)), dma((2,)), dma((2,)),
        ],
        compiler_params=pltpu.CompilerParams(
            collective_id=0, has_side_effects=True, vmem_limit_bytes=24 << 20
        ),
    )(vectors, pre, thickness, foundation, patch_rows, matched, elem)


def solution(mesh):
    split = ("groups", "patch", "sub", "half")
    in_specs = (
        P(None, split, None),
        P(split, None, None),
        P(split, None),
        P(split, None),
        P(split),
        P(split),
        P(split),
    )
    return jax.shard_map(
        per_device, mesh=mesh, in_specs=in_specs, out_specs=P(None, split, None), check_vma=False
    )
```

time: 212 us -> 37.1 us (0.18)
  local copies, waits for them, and re-layouts: 75.2 us -> 5.43 us
  blocking collectives: 59.7 us -> 0 us
  Pallas kernels: 0 us -> 31.4 us
  starting transfers between devices: 26.3 us -> 0 us
  waiting for transfers between devices: 26 us -> 0 us
  between operations: 13.6 us -> 0.02 us
  other arithmetic: 10.3 us -> 0 us
    psum x2 -> x0, blocking collectives: 59.7 us -> none  [per_device(): totals = lax.psum(products(field, kfield, gfield), ('patch', 'sub', 'half'))]
    gather x4 -> x0, local copies, waits for them, and re-layouts: 49.2 us -> none  [row_pick(): return jnp.take_along_axis(field, where_rows, axis=2)[:, :, 0, :]]
    pallas_call x0 -> x1, Pallas kernels: none -> 31.4 us  [per_device(): pl.pallas_call(body, out_shape=jax.ShapeDtypeStruct((2, rows_dev, ncol),...]
    all_to_all x4 -> x0, waiting for transfers between devices: 24.9 us -> none  [the longest x1 11.4 us: per_device(): lax.all_to_all(blocks, 'patch', split_axis=0, concat_axis=0, tiled=True)]
    all_to_all x4 -> x0, starting transfers between devices: 13.4 us -> none  [the longest x1 3.46 us: per_device(): lax.all_to_all(blocks, 'patch', split_axis=0, concat_axis=0, tiled=True)]
    ppermute x6 -> x0, starting transfers between devices: 12.9 us -> none  [passed_along(): lax.ppermute(array, axis, [(i, (i + by) % peers) for i in range(peers)])]
    another operation x6 -> x0, local copies, waits for them, and re-layouts: 7.64 us -> none  [the longest x2 7.63 us: products(): jnp.stack([jnp.sum(field[0] * kfield[0]), jnp.sum(field[0] * kfield[1]),...]
    scatter x1 -> x0, local copies, waits for them, and re-layouts: 6.97 us -> none  [per_device(): placed = jnp.zeros((rows_dev, 3, ncol), jnp.bfloat16).at[arrived_rows.res...]
  transfers between devices with their start and end apart: 10 -> 0, of which waited for: 5 -> 0; matrix products, arithmetic and copies ran while one was open for 2% -> 0% of each run, Pallas kernels for 0% -> 0%
where the time goes in v1:
time: 37.1 us; the launch traced here: 36.9 us
  Pallas kernels  31.4 us (85%)
  local copies, waits for them, and re-layouts  5.43 us (15%)
    pallas_call x1, Pallas kernels, per_device(): pl.pallas_call(body, out_shape=jax.ShapeDtypeStruct((2, rows_dev, ncol),...  31.4 us
    unnamed x15, local copies, waits for them, and re-layouts  5.43 us

profile of v1, /device:TPU:0, one launch (start us, length us, event | category | flops | bytes accessed | tf_op | source)
XLA Modules:
  0.0 36.9 jit_solution(17657877414276254510)
XLA Ops:
  0.0 0.0 copy-start.6
  0.0 0.0 copy-start.4
  0.0 0.0 copy-start.5
  0.0 0.6 %copy-done.6 = s32[2]{0:T(128)S(1)} copy-done((s32[2]{0:T(128)S(1)}, s32[2]{0:T(128)}, u32[]{:S(2)}) %copy-start.6) | copy-done | bytes 32
  0.7 0.0 copy-done.4
  0.7 0.0 copy-done.5
  0.7 0.0 copy-start
  0.7 1.0 %copy-done = f32[2,256,256]{2,1,0:T(8,128)S(1)} copy-done((f32[2,256,256]{2,1,0:T(8,128)S(1)}, f32[2,256,256]{2,1,0:T(8,128)}, u32[]{:S(2)}) %copy-start) | copy-done | bytes 524312
  1.7 0.0 copy-start.1
  1.7 1.0 %copy-done.1 = bf16[256,3,256]{2,0,1:T(8,128)(2,1)S(1)} copy-done((bf16[256,3,256]{2,0,1:T(8,128)(2,1)S(1)}, bf16[256,3,256]{2,0,1:T(8,128)(2,1)}, u32[]{:S(2)}) %copy-start.1) | copy-done | bytes 393240
  2.7 0.0 copy-start.2
  2.7 0.9 %copy-done.2 = f32[256,256]{1,0:T(8,128)S(1)} copy-done((f32[256,256]{1,0:T(8,128)S(1)}, f32[256,256]{1,0:T(8,128)}, u32[]{:S(2)}) %copy-start.2) | copy-done | bytes 262168
  3.7 0.0 copy-start.3
  3.7 0.9 %copy-done.3 = f32[256,256]{1,0:T(8,128)S(1)} copy-done((f32[256,256]{1,0:T(8,128)S(1)}, f32[256,256]{1,0:T(8,128)}, u32[]{:S(2)}) %copy-start.3) | copy-done | bytes 262168
  4.6 31.4 %shard_map.73 = f32[2,256,256]{2,1,0:T(8,128)S(1)} custom-call(f32[2,256,256]{2,1,0:T(8,128)S(1)} %copy-done, bf16[3,16,16,256]{3,2,1,0:T(8,128)(2,1)S(1)} %bitcast.4, f32[256,256]{1,0:T(8,128)S(1)} %copy-done.2, f32[256,256]{1,0:T(8,128)S(1)} %copy-done.3, s32[2]{0:T(128)S(1)} %copy-done.5, s32[2]{0:T(128)S(1)} %copy-done.6, s32[1,256]{1,0:T(1,128)S(1)} %bitcast.5), custom_call_target="tpu_custom_call" | custom-call | tf_op jit(solution)/shard_map/pallas_call | solution.py:466
  36.1 0.8 %copy.9 = f32[2,256,256]{2,1,0:T(8,128)} copy(f32[2,256,256]{2,1,0:T(8,128)S(1)} %shard_map.73) | data formatting | bytes 1048576
Async XLA Ops:
  0.0 0.7 %copy-start.6 = (s32[2]{0:T(128)S(1)}, s32[2]{0:T(128)}, u32[]{:S(2)}) copy-start(s32[2]{0:T(128)} %matched.1) | copy-start | bytes 28
  0.0 0.7 %copy-start.4 = (s32[256]{0:T(256)S(1)}, s32[256]{0:T(256)}, u32[]{:S(2)}) copy-start(s32[256]{0:T(256)} %param.13) | copy-start | bytes 3076
  0.0 0.7 %copy-start.5 = (s32[2]{0:T(128)S(1)}, s32[2]{0:T(128)}, u32[]{:S(2)}) copy-start(s32[2]{0:T(128)} %lengths.1) | copy-start | bytes 28
  0.7 1.0 %copy-start = (f32[2,256,256]{2,1,0:T(8,128)S(1)}, f32[2,256,256]{2,1,0:T(8,128)}, u32[]{:S(2)}) copy-start(f32[2,256,256]{2,1,0:T(8,128)} %vec.1) | copy-start | bytes 1572868
  1.7 1.0 %copy-start.1 = (bf16[256,3,256]{2,0,1:T(8,128)(2,1)S(1)}, bf16[256,3,256]{2,0,1:T(8,128)(2,1)}, u32[]{:S(2)}) copy-start(bf16[256,3,256]{2,0,1:T(8,128)(2,1)} %param.8) | copy-start | bytes 1179652
  2.7 0.9 %copy-start.2 = (f32[256,256]{1,0:T(8,128)S(1)}, f32[256,256]{1,0:T(8,128)}, u32[]{:S(2)}) copy-start(f32[256,256]{1,0:T(8,128)} %thick_in.1) | copy-start | bytes 786436
  3.7 0.9 %copy-start.3 = (f32[256,256]{1,0:T(8,128)S(1)}, f32[256,256]{1,0:T(8,128)}, u32[]{:S(2)}) copy-start(f32[256,256]{1,0:T(8,128)} %found_in.1) | copy-start | bytes 786436

commit v2 on v1

--- a/solution.py
+++ b/solution.py
@@ -13,11 +13,12 @@
 MESH = pl.DeviceIdType.MESH
 PAD = 8
 LANES = 128
-CHUNK = 32
+CHUNK = 128
 
 
 def body(
-    vec, pre, thick_in, found_in, lengths, matched, elem, out,
+    vec, pre, thick_in, found_in, lengths_in, matched_in, elem, out,
+    lengths, matched,
     x, thick, found, prec, stress, mrow, frow, kpart, gpart, kf, gf,
     arrived, ids, strips, got, edge, sums, coef,
     load_sem, own_sem, data_send, data_recv, ids_send, ids_recv,
@@ -36,21 +37,38 @@
     per_slot = prows // chunk
     steps = slots * per_slot
 
+    ends_of = 2 if owners % 2 == 0 else 1
+    near = owners // ends_of
+
     def peer(d):
-        k = lax.rem(me + d, n)
-        where = {
-            "patch": lax.div(k, subs * halves),
-            "sub": lax.rem(lax.div(k, halves), subs),
-            "half": lax.rem(k, halves),
-        }
-        return k, where
+        step = lax.rem(d + (n // 2 if ends_of == 2 else 0), n)
+        side = lax.rem(lax.div(pi, near) + lax.div(step, near * subs * halves), ends_of)
+        along = lax.rem(lax.rem(pi, near) + lax.rem(lax.div(step, subs * halves), near), near)
+        to_patch = side * near + along
+        to_sub = lax.rem(si + lax.rem(lax.div(step, halves), subs), subs)
+        to_half = lax.rem(hi + lax.rem(step, halves), halves)
+        k = (to_patch * subs + to_sub) * halves + to_half
+        return k, {"patch": to_patch, "sub": to_sub, "half": to_half}
+
+    def for_peers(action):
+        start = n // 2 if ends_of == 2 else 0
+
+        def one(e):
+            d = lax.select(e < start, e, e + 1) if start else e + 1
+            action(*peer(d))
+
+        if n <= 16:
+            for e in range(n - 1):
+                one(jnp.int32(e))
+        else:
+            pl.loop(0, n - 1)(one)
 
     barrier = pltpu.get_barrier_semaphore()
 
-    @pl.loop(1, n)
-    def _(d):
-        _, where = peer(d)
+    def greet(k, where):
         pl.semaphore_signal(barrier, inc=1, device_id=where, device_id_type=MESH)
+
+    for_peers(greet)
 
     loads = []
     for v in range(2):
@@ -66,7 +84,11 @@
     load_found = pltpu.make_async_copy(found_in, found, load_sem.at[2 * slots + 1])
     own_data = pltpu.make_async_copy(pre.at[:, me], arrived.at[:, me], own_sem.at[0])
     own_ids = pltpu.make_async_copy(elem, ids.at[me], own_sem.at[1])
-    for copy in loads + [load_thick, load_found, own_data, own_ids]:
+    load_ints = [
+        pltpu.make_async_copy(lengths_in, lengths, own_sem.at[2]),
+        pltpu.make_async_copy(matched_in, matched, own_sem.at[3]),
+    ]
+    for copy in load_ints + loads + [load_thick, load_found, own_data, own_ids]:
         copy.start()
 
     zero_pad = jnp.zeros((PAD, ncol), jnp.float32)
@@ -75,7 +97,7 @@
             for ref in (x, mrow, frow):
                 ref[v, s, 0:PAD, :] = zero_pad
                 ref[v, s, PAD + prows : 2 * PAD + prows, :] = zero_pad
-    for copy in loads:
+    for copy in load_ints + loads:
         copy.wait()
 
     def fill_strip(which, row_of):
@@ -114,9 +136,7 @@
     for copy in first_strips:
         copy.start()
 
-    @pl.loop(1, n)
-    def _(d):
-        k, where = peer(d)
+    def send_block(k, where):
         pltpu.make_async_remote_copy(
             src_ref=elem, dst_ref=ids.at[me], send_sem=ids_send.at[0],
             recv_sem=ids_recv.at[0], device_id=where, device_id_type=MESH,
@@ -125,6 +145,8 @@
             src_ref=pre.at[:, k], dst_ref=arrived.at[:, me], send_sem=data_send.at[0],
             recv_sem=data_recv.at[0], device_id=where, device_id_type=MESH,
         ).start()
+
+    for_peers(send_block)
 
     def all_ids():
         part = ids.at[pl.ds(0, n - 1)]
@@ -301,10 +323,10 @@
             line = jnp.where(spot == t, one, line)
         sums[it, me] = line
 
-        @pl.loop(1, n)
-        def _(d):
-            _, where = peer(d)
+        def send_line(k, where):
             sum_copy(it, where).start()
+
+        for_peers(send_line)
 
     def read_sums(it):
         all_sums(it).wait_recv()
@@ -460,15 +482,16 @@
     flat = pltpu.VMEM((rows_dev, ncol), f32)
     pair = pltpu.VMEM((2, rows_dev, ncol), f32)
     strip_rows = slots * 8 + -(-slots // 8) * 8
-    anywhere = pl.BlockSpec(memory_space=pl.ANY)
-    scalars = pl.BlockSpec(memory_space=pltpu.SMEM)
+    hbm = pl.BlockSpec(memory_space=pltpu.HBM)
     dma = pltpu.SemaphoreType.DMA
+    operands = (vectors, pre, thickness, foundation, patch_rows, matched, elem)
     return pl.pallas_call(
         body,
         out_shape=jax.ShapeDtypeStruct((2, rows_dev, ncol), f32),
-        in_specs=[anywhere] * 4 + [scalars] * 2 + [anywhere],
+        in_specs=[hbm] * 7,
         out_specs=pl.BlockSpec(memory_space=pltpu.VMEM),
         scratch_shapes=[
+            pltpu.SMEM((slots,), jnp.int32), pltpu.SMEM((slots,), jnp.int32),
             padded, flat, flat, flat,
             pltpu.VMEM((3, rows_dev, ncol), f32),
             padded, padded, pair, pair, pair, pair,
@@ -479,14 +502,14 @@
             pltpu.VMEM((slots, 2, 8, ncol), f32),
             pltpu.VMEM((2, n, 1, LANES), f32),
             pltpu.VMEM((8, ncol), f32),
-            dma((2 * slots + 2,)), dma((2,)),
+            dma((2 * slots + 2,)), dma((4,)),
             dma((1,)), dma((1,)), dma((1,)), dma((1,)),
             dma((6,)), dma((6,)), dma((2,)), dma((2,)),
         ],
         compiler_params=pltpu.CompilerParams(
             collective_id=0, has_side_effects=True, vmem_limit_bytes=24 << 20
         ),
-    )(vectors, pre, thickness, foundation, patch_rows, matched, elem)
+    )(*(pltpu.with_memory_space_constraint(a, pltpu.HBM) for a in operands))
 
 
 def solution(mesh):

time: 37.1 us -> 30.3 us (0.82)
  local copies, waits for them, and re-layouts: 5.43 us -> 0.8 us
  Pallas kernels: 31.4 us -> 29.4 us
    unnamed x15 -> x1, local copies, waits for them, and re-layouts: 5.43 us -> 0.8 us
    pallas_call x1, Pallas kernels: 31.4 us -> 29.4 us  [per_device(): pl.pallas_call(body, out_shape=jax.ShapeDtypeStruct((2, rows_dev, ncol),...]
where the time goes in v2:
time: 30.3 us; the launch traced here: 30.2 us
  Pallas kernels  29.4 us (97%)
  local copies, waits for them, and re-layouts  0.8 us (3%)
    pallas_call x1, Pallas kernels, per_device(): pl.pallas_call(body, out_shape=jax.ShapeDtypeStruct((2, rows_dev, ncol),...  29.4 us
    unnamed x1, local copies, waits for them, and re-layouts  0.8 us

profile of v2, /device:TPU:0, one launch (start us, length us, event | category | flops | bytes accessed | tf_op | source)
XLA Modules:
  0.0 30.2 jit_solution(16349331952050357909)
XLA Ops:
  0.0 29.4 %shard_map.73 = f32[2,256,256]{2,1,0:T(8,128)S(1)} custom-call(f32[2,256,256]{2,1,0:T(8,128)} %vec.1, bf16[3,16,16,256]{3,2,1,0:T(8,128)(2,1)} %bitcast.4, f32[256,256]{1,0:T(8,128)} %thick_in.1, f32[256,256]{1,0:T(8,128)} %found_in.1, s32[2]{0:T(128)} %lengths_in.1, s32[2]{0:T(128)} %matched_in.1, s32[1,256]{1,0:T(1,128)} %bitcast.5), custom_call_target="tpu_custom_call" | custom-call | tf_op jit(solution)/shard_map/pallas_call | solution.py:488
  29.4 0.8 %copy.9 = f32[2,256,256]{2,1,0:T(8,128)} copy(f32[2,256,256]{2,1,0:T(8,128)S(1)} %shard_map.73) | data formatting | bytes 1048576

commit v3 on v2

--- a/solution.py
+++ b/solution.py
@@ -20,7 +20,7 @@
     vec, pre, thick_in, found_in, lengths_in, matched_in, elem, out,
     lengths, matched,
     x, thick, found, prec, stress, mrow, frow, kpart, gpart, kf, gf,
-    arrived, ids, strips, got, edge, sums, coef,
+    arrived, ids, strips, got, kept, edge, sums, coef,
     load_sem, own_sem, data_send, data_recv, ids_send, ids_recv,
     strip_send, strip_recv, sum_send, sum_recv,
 ):
@@ -186,7 +186,7 @@
     load_thick.wait()
     load_found.wait()
 
-    @pl.loop(0, steps)
+    @pl.loop(0, steps, unroll=True)
     def _(i):
         s, r0, full, row, length = place(i)
         live = row < length
@@ -284,6 +284,10 @@
                 label = got[0, side, rows_strip + t : rows_strip + t + 1, :]
                 top = top + jnp.where(label == mine, got[which, side, base : base + 2, :], 0.0)
         return top, bottom
+
+    def keep(which, s, v, top, bottom):
+        kept[which, s, v, 0:2, :] = top
+        kept[which, s, v, 2:4, :] = bottom
 
     def set_edge(s, v, partner_top, partner_bottom):
         length = jnp.maximum(lengths[s], 2)
@@ -315,12 +319,14 @@
             device_id={"patch": pi}, device_id_type=MESH,
         )
 
-    def send_sums(it, totals):
+    def put_sums(line, first, totals):
         spot = lax.broadcasted_iota(jnp.int32, (1, LANES), 1)
-        line = jnp.zeros((1, LANES), jnp.float32)
-        for t, total in enumerate(totals):
+        for t, total in enumerate(totals, first):
             one = jnp.sum(jnp.sum(total, axis=0, keepdims=True), axis=1, keepdims=True)
             line = jnp.where(spot == t, one, line)
+        return line
+
+    def send_sums(it, line):
         sums[it, me] = line
 
         def send_line(k, where):
@@ -372,13 +378,16 @@
 
     nothing = tuple(jnp.zeros((8, ncol), jnp.float32) for _ in range(3))
 
-    pl.loop(0, steps)(stiff_first)
+    pl.loop(0, steps, unroll=True)(stiff_first)
     for copy in first_strips:
         copy.wait_recv()
     for s in range(slots):
         for v in range(2):
-            set_edge(s, v, *chosen(0, v, s))
-    k_sums = lax.fori_loop(0, steps, stiff_second, nothing)
+            top, bottom = chosen(0, v, s)
+            keep(0, s, v, top, bottom)
+            set_edge(s, v, top, bottom)
+    no_line = jnp.zeros((1, LANES), jnp.float32)
+    k_line = put_sums(no_line, 0, lax.fori_loop(0, steps, stiff_second, nothing, unroll=True))
 
     def scaled_row(ref):
         def pick(s, v, at):
@@ -417,45 +426,48 @@
             onehot, block, (((0,), (0,)), ((), ())), preferred_element_type=jnp.float32
         )
 
-    pl.loop(0, steps)(geo_first)
-    g_sums = lax.fori_loop(0, steps, geo_second, nothing)
-    send_sums(0, k_sums + g_sums)
+    pl.loop(0, steps, unroll=True)(geo_first)
+    g_sums = lax.fori_loop(0, steps, geo_second, nothing, unroll=True)
+    send_sums(0, put_sums(k_line, 3, g_sums))
     fill_strip(2, scaled_row(gf))
     third_strips = strip_copies(2, rows_strip)
     for copy in third_strips:
         copy.start()
 
+    for copy in second_strips:
+        copy.wait_recv()
+    for s in range(slots):
+        for v in range(2):
+            keep(1, s, v, *chosen(1, v, s))
     read_sums(0)
 
-    @pl.loop(0, steps)
+    @pl.loop(0, steps, unroll=True)
     def _(i):
         s, r0, full, new0, new1 = advanced(i)
         x[0, s, pl.ds(r0 + PAD, chunk), :] = new0
         x[1, s, pl.ds(r0 + PAD, chunk), :] = new1
 
-    @pl.loop(0, steps)
+    @pl.loop(0, steps, unroll=True)
     def _(i):
         stiff_first(i)
         geo_first(i)
 
-    for copy in second_strips + third_strips:
+    for copy in third_strips:
         copy.wait_recv()
     for s in range(slots):
-        parts = [[chosen(which, v, s) for v in range(2)] for which in range(3)]
-        ends = []
-        for end in range(2):
-            ends.append(stepped(*(parts[which][v][end] for which in range(3) for v in range(2))))
-        for v in range(2):
-            set_edge(s, v, ends[0][v], ends[1][v])
+        last = [jnp.concatenate(chosen(2, v, s), axis=0) for v in range(2)]
+        ends = stepped(*(kept[which, s, v, 0:4, :] for which in range(2) for v in range(2)), *last)
+        for v in range(2):
+            set_edge(s, v, ends[v][0:2], ends[v][2:4])
 
     def second(i, acc):
         return stiff_second(i, acc[:3]) + geo_second(i, acc[3:])
 
-    totals = lax.fori_loop(0, steps, second, nothing + nothing)
-    send_sums(1, totals)
+    totals = lax.fori_loop(0, steps, second, nothing + nothing, unroll=True)
+    send_sums(1, put_sums(no_line, 0, totals))
     read_sums(1)
 
-    @pl.loop(0, steps)
+    @pl.loop(0, steps, unroll=True)
     def _(i):
         s, r0, full, new0, new1 = advanced(i)
         out[0, full, :] = new0
@@ -499,6 +511,7 @@
             pltpu.VMEM((n, 1, rows_dev), jnp.int32),
             pltpu.VMEM((3, strip_rows, ncol), f32),
             pltpu.VMEM((3, 2, strip_rows, ncol), f32),
+            pltpu.VMEM((2, slots, 2, 8, ncol), f32),
             pltpu.VMEM((slots, 2, 8, ncol), f32),
             pltpu.VMEM((2, n, 1, LANES), f32),
             pltpu.VMEM((8, ncol), f32),

time: 30.3 us -> 29.6 us (0.977)
  Pallas kernels: 29.4 us -> 28.7 us
    pallas_call x1, Pallas kernels: 29.4 us -> 28.7 us  [per_device(): pl.pallas_call(body, out_shape=jax.ShapeDtypeStruct((2, rows_dev, ncol),...]
where the time goes in v3:
time: 29.6 us; the launch traced here: 29.5 us
  Pallas kernels  28.7 us (97%)
  local copies, waits for them, and re-layouts  0.8 us (3%)
    pallas_call x1, Pallas kernels, per_device(): pl.pallas_call(body, out_shape=jax.ShapeDtypeStruct((2, rows_dev, ncol),...  28.7 us
    unnamed x1, local copies, waits for them, and re-layouts  0.8 us

profile of v3, /device:TPU:0, one launch (start us, length us, event | category | flops | bytes accessed | tf_op | source)
XLA Modules:
  0.0 29.5 jit_solution(17161412493477133127)
XLA Ops:
  0.0 28.7 %shard_map.73 = f32[2,256,256]{2,1,0:T(8,128)S(1)} custom-call(f32[2,256,256]{2,1,0:T(8,128)} %vec.1, bf16[3,16,16,256]{3,2,1,0:T(8,128)(2,1)} %bitcast.4, f32[256,256]{1,0:T(8,128)} %thick_in.1, f32[256,256]{1,0:T(8,128)} %found_in.1, s32[2]{0:T(128)} %lengths_in.1, s32[2]{0:T(128)} %matched_in.1, s32[1,256]{1,0:T(1,128)} %bitcast.5), custom_call_target="tpu_custom_call" | custom-call | tf_op jit(solution)/shard_map/pallas_call | solution.py:500
  28.7 0.8 %copy.9 = f32[2,256,256]{2,1,0:T(8,128)} copy(f32[2,256,256]{2,1,0:T(8,128)S(1)} %shard_map.73) | data formatting | bytes 1048576

commit v4 on v3

--- a/solution.py
+++ b/solution.py
@@ -398,8 +398,6 @@
 
     fill_strip(1, scaled_row(kf))
     second_strips = strip_copies(1, rows_strip)
-    for copy in second_strips:
-        copy.start()
 
     own_ids.wait()
     all_ids().wait_recv()
@@ -416,6 +414,8 @@
 
     own_data.wait()
     all_data().wait_recv()
+    for copy in second_strips:
+        copy.start()
     for c in range(3):
         block = arrived[c]
         if per_peer % 8:

time: 29.6 us -> 29.1 us (0.983)
  Pallas kernels: 28.7 us -> 28.2 us
    pallas_call x1, Pallas kernels: 28.7 us -> 28.2 us  [per_device(): pl.pallas_call(body, out_shape=jax.ShapeDtypeStruct((2, rows_dev, ncol),...]
where the time goes in v4:
time: 29.1 us; the launch traced here: 29 us
  Pallas kernels  28.2 us (97%)
  local copies, waits for them, and re-layouts  0.8 us (3%)
    pallas_call x1, Pallas kernels, per_device(): pl.pallas_call(body, out_shape=jax.ShapeDtypeStruct((2, rows_dev, ncol),...  28.2 us
    unnamed x1, local copies, waits for them, and re-layouts  0.8 us

profile of v4, /device:TPU:0, one launch (start us, length us, event | category | flops | bytes accessed | tf_op | source)
XLA Modules:
  0.0 29.0 jit_solution(1171002710847936019)
XLA Ops:
  0.0 28.2 %shard_map.73 = f32[2,256,256]{2,1,0:T(8,128)S(1)} custom-call(f32[2,256,256]{2,1,0:T(8,128)} %vec.1, bf16[3,16,16,256]{3,2,1,0:T(8,128)(2,1)} %bitcast.4, f32[256,256]{1,0:T(8,128)} %thick_in.1, f32[256,256]{1,0:T(8,128)} %found_in.1, s32[2]{0:T(128)} %lengths_in.1, s32[2]{0:T(128)} %matched_in.1, s32[1,256]{1,0:T(1,128)} %bitcast.5), custom_call_target="tpu_custom_call" | custom-call | tf_op jit(solution)/shard_map/pallas_call | solution.py:500
  28.2 0.8 %copy.9 = f32[2,256,256]{2,1,0:T(8,128)} copy(f32[2,256,256]{2,1,0:T(8,128)S(1)} %shard_map.73) | data formatting | bytes 1048576
